TPU v7x, 32 devices: a whole 2x2x4 slice. The times are simulated.
32 devices in a mesh: group: 2 (over x), expert: 16 (over z, y, core), tensor: 1.
Axes of the slice: x: 2, y: 2, z: 4, core: 2. Of those that a mesh axis runs over, the one named last changes fastest.
Arguments:
- tokens: bfloat16 [1024, 4096], P(('group', 'expert', 'tensor')), parts along dimension 0, may hold values from -600 to 600
- norm_gain: float32 [4096], replicated, may hold values from 0.1 to 1.9
- w_gate: bfloat16 [16, 4096, 768], P('expert', None, 'tensor'), may hold values from -0.09375 to 0.09375
- w_up: bfloat16 [16, 4096, 768], P('expert', None, 'tensor'), may hold values from -0.09375 to 0.09375
- w_down: bfloat16 [16, 768, 4096], P('expert', 'tensor'), may hold values from -0.4375 to 0.4375
- expert_ids: int32 [1024, 8], P(('group', 'expert', 'tensor')), parts along dimension 0, may hold values from 0 to 15, all different within a row; in each aligned block of 32 rows (0 to 31, 32 to 63, ...) at most 32 rows name the same one
- route_weights: float32 [1024, 8], P(('group', 'expert', 'tensor')), parts along dimension 0, may hold values from 0.05 to 1
Outputs:
- mixed: bfloat16 [1024, 4096], P(('group', 'expert', 'tensor')), parts along dimension 0
There are 2 independent parts, one for each index of `group`. A program takes and returns all parts, laid end to end along the dimension named above; an argument that names none is the same for every part. Nothing has to cross between parts.
Inputs may be any that keep to these rules, and one draw needn't show every extreme that they name: `expert_ids`: each row names 8 different experts. Among the 32 rows of one device no expert is named more than 32 times, and in every draw some device names some expert exactly 32 times.
All inputs are finite; a program needn't handle non-finite values.
Results may differ from a plain program's by a relative error of at most 0.0077.
Values may be sent and summed in bfloat16 or wider, within the bound.
A program may use at most 128 MiB of HBM per device.

v0:
```python
import jax
import jax.numpy as jnp
from jax import lax
from jax.sharding import PartitionSpec as P

epsilon = 1e-06


def shards(tokens, norm_gain, w_gate, w_up, w_down, expert_ids, route_weights):
    row_count, feature_count = tokens.shape
    pick_count = expert_ids.shape[1]
    experts = lax.axis_size("expert")
    pair_size = lax.axis_size("tensor")
    capacity = min(row_count, 2 * row_count * pick_count // experts)
    stream = tokens.astype(jnp.float32)
    normed = (
        stream * lax.rsqrt(jnp.mean(stream * stream, axis=-1, keepdims=True) + epsilon) * norm_gain
    ).astype(jnp.bfloat16)
    route = route_weights / jnp.sum(route_weights, axis=-1, keepdims=True)
    flat_ids = expert_ids.reshape(-1)
    onehot = (flat_ids[:, None] == jnp.arange(experts, dtype=jnp.int32)[None, :]).astype(jnp.int32)
    slot_index = jnp.sum((jnp.cumsum(onehot, axis=0) - 1) * onehot, axis=1)
    target = flat_ids * capacity + slot_index
    slot_range = jnp.arange(experts * capacity, dtype=jnp.int32)
    placing = (slot_range[:, None] == target[None, :]).reshape(
        experts * capacity, row_count, pick_count
    )
    send_matrix = jnp.sum(placing.astype(jnp.float32), axis=2).astype(jnp.bfloat16)
    sendbuf = jnp.dot(send_matrix, normed, preferred_element_type=jnp.float32).astype(jnp.bfloat16)
    sendbuf = sendbuf.reshape(experts, 1, capacity, feature_count)
    gathering = (target[:, None] == slot_range[None, :]).reshape(
        row_count, pick_count, experts * capacity
    )
    combine_matrix = jnp.sum(gathering.astype(jnp.float32) * route[:, :, None], axis=1)
    copies = jnp.broadcast_to(sendbuf, (experts, pair_size, capacity, feature_count)).reshape(
        experts * pair_size, capacity, feature_count
    )
    arrived = lax.all_to_all(copies, ("expert", "tensor"), split_axis=0, concat_axis=0, tiled=True)
    incoming = arrived.reshape(experts, pair_size, capacity, feature_count)
    row_block = incoming.reshape(-1, feature_count)
    gate_pre = jnp.dot(row_block, w_gate[0], preferred_element_type=jnp.float32)
    up_pre = jnp.dot(row_block, w_up[0], preferred_element_type=jnp.float32)
    hidden = (jax.nn.silu(gate_pre) * up_pre).astype(jnp.bfloat16)
    partial_value = jnp.dot(hidden, w_down[0], preferred_element_type=jnp.float32)
    bring_partial_value = partial_value.astype(jnp.bfloat16).reshape(
        incoming.shape[:3] + (feature_count,)
    )
    slots_here = bring_partial_value.shape[2]
    summed = (
        lax.psum_scatter(bring_partial_value, "tensor", scatter_dimension=1, tiled=True)
        .astype(jnp.float32)
        .astype(jnp.bfloat16)
    )
    returned_rows = lax.all_to_all(summed, "expert", split_axis=0, concat_axis=0, tiled=True)
    returned = returned_rows.reshape(experts, slots_here, feature_count)
    widened = returned.reshape(experts * capacity, feature_count).astype(jnp.float32)
    mixed = jnp.dot(
        combine_matrix, widened, precision=lax.Precision.HIGHEST, preferred_element_type=jnp.float32
    )
    return mixed.astype(jnp.bfloat16)


def solution(mesh):
    in_specs = (
        P(("group", "expert", "tensor"), None),
        P(),
        P("expert", None, "tensor"),
        P("expert", None, "tensor"),
        P("expert", "tensor", None),
        P(("group", "expert", "tensor"), None),
        P(("group", "expert", "tensor"), None),
    )
    out_specs = P(("group", "expert", "tensor"), None)
    return jax.shard_map(shards, mesh=mesh, in_specs=in_specs, out_specs=out_specs, check_vma=False)
```

profile of v0, /device:TPU:13, one launch (start us, length us, event | category | flops | bytes accessed | tf_op | source)
XLA Modules:
  0.0 229.2 jit_solution(13112026851367182960)
XLA Ops:
  0.0 0.8 copy.22
  0.8 0.1 eq.57
  0.9 0.1 eq.53
  1.0 0.6 reduce-window.6
  1.5 0.2 slice_reduce_fusion
  1.8 0.1 fusion.21
  1.9 0.1 reduce_sum.48
  2.0 0.2 convert_reduce_fusion
  2.2 1.1 fusion.13
  3.3 0.0 slice-start
  3.3 2.4 %convolution_convert_fusion = bf16[512,4096]{1,0:T(8,128)(2,1)S(1)} fusion(bf16[32,4096]{1,0:T(8,128)(2,1)} %param.7, f32[4096]{0:T(1024)} %param.8, f32[32]{0:T(128)S(1)} %add_rsqrt_fusion, bf16[512,32]{0,1:T(8,128)(2,1)S(1)} %convert_reduce_fusion), kind=kOutput, calls=%fused_computation.7 | convolution fusion | flops 136839168 | bytes 4505728 | tf_op jit(solution)/shard_map/dot_general | solution.py:29
  5.7 0.0 slice-start.1
  5.8 98.7 %all_to_all.10 = bf16[16,32,4096]{2,1,0:T(8,128)(2,1)S(1)} all-to-all(bf16[16,32,4096]{2,1,0:T(8,128)(2,1)S(1)} %bitcast.41), channel_id=1, replica_groups=mesh['group'=2,'expert'=16,'tensor'=1] {'expert','tensor'}, dimensions={0} | all-to-all | bytes 8388608 | tf_op jit(solution)/shard_map/all_to_all | solution.py:38
  104.4 0.0 copy-start
  104.4 2.0 copy-done
  106.4 0.0 slice-done
  106.4 0.0 slice-done.1
  106.4 3.4 %fusion.4 = f32[512,768]{1,0:T(8,128)S(1)} fusion(bf16[512,4096]{1,0:T(8,128)(2,1)S(1)} %bitcast.43, bf16[1,4096,768]{2,1,0:T(8,128)(2,1)S(1)} %bitcast.46), kind=kOutput, calls=%fused_computation.4 | convolution fusion | flops 3221225472 | bytes 12058624 | tf_op jit(solution)/shard_map/dot_general | solution.py:41
  109.8 16.5 %fusion.6 = bf16[512,4096]{1,0:T(8,128)(2,1)} fusion(bf16[1,768,4096]{2,1,0:T(8,128)(2,1)} %param.11, f32[512,768]{1,0:T(8,128)S(1)} %fusion.4, bf16[512,4096]{1,0:T(8,128)(2,1)} %bitcast.44, bf16[1,4096,768]{2,1,0:T(8,128)(2,1)} %param.10), kind=kOutput, calls=%fused_computation.6 | convolution fusion | flops 6446907392 | bytes 22544384 | tf_op jit(solution)/shard_map/dot_general | solution.py:44
  126.4 0.0 copy-start.1
  126.4 5.3 %all-to-all-start.1 = ((bf16[16,1,32,4096]{3,2,1,0:T(8,128)(2,1)}), bf16[16,1,32,4096]{3,2,1,0:T(8,128)(2,1)}, u32[]{:S(2)}, u32[]{:S(2)}) async-start(bf16[16,1,32,4096]{3,2,1,0:T(8,128)(2,1)} %bitcast.42), calls=%async_computation.1 | async-start | bytes 8388608 | tf_op jit(solution)/shard_map/all_to_all | solution.py:54
  131.7 0.0 copy-done.1
  131.8 0.1 copy.26
  131.8 0.2 select_reduce_fusion
  132.1 92.1 %all-to-all-done.1 = bf16[16,1,32,4096]{3,2,1,0:T(8,128)(2,1)} async-done(((bf16[16,1,32,4096]{3,2,1,0:T(8,128)(2,1)}), bf16[16,1,32,4096]{3,2,1,0:T(8,128)(2,1)}, u32[]{:S(2)}, u32[]{:S(2)}) %all-to-all-start.1) | async-done | bytes 4194336 | tf_op jit(solution)/shard_map/all_to_all | solution.py:54
  224.2 5.0 %convolution_convert_fusion.1 = bf16[32,4096]{1,0:T(8,128)(2,1)} fusion(f32[32,512]{1,0:T(8,128)S(1)} %select_reduce_fusion, bf16[512,4096]{1,0:T(8,128)(2,1)} %bitcast.8), kind=kOutput, calls=%fused_computation.8 | convolution fusion | flops 805437440 | bytes 4521984 | tf_op jit(solution)/shard_map/dot_general | solution.py:57
  (8 shorter events, 0.1 us)
Async XLA Ops:
  3.3 103.1 %slice-start = ((s8[6291456]{0:T(1024)(128)(4,1)}), s8[4194304]{0:T(1024)(128)(4,1)S(1)}, s32[]{:S(2)}) async-start(s8[6291456]{0:T(1024)(128)(4,1)} %bitcast.45), calls=%async_computation.2 | async-start | bytes 8388608
  5.7 100.7 %slice-start.1 = ((s8[6291456]{0:T(1024)(128)(4,1)}), s8[2097152]{0:T(1024)(128)(4,1)S(1)}, s32[]{:S(2)}) async-start(s8[6291456]{0:T(1024)(128)(4,1)} %bitcast.45), calls=%async_computation.3 | async-start | bytes 4194304
  104.4 2.0 copy-start
  126.4 5.3 %copy-start.1 = (f32[32,8]{0,1:T(8,128)S(1)}, f32[32,8]{0,1:T(8,128)}, u32[]{:S(2)}) copy-start(f32[32,8]{0,1:T(8,128)} %param.13) | copy-start | bytes 3076
  126.4 97.8 %all-to-all-start.1 = ((bf16[16,1,32,4096]{3,2,1,0:T(8,128)(2,1)}), bf16[16,1,32,4096]{3,2,1,0:T(8,128)(2,1)}, u32[]{:S(2)}, u32[]{:S(2)}) async-start(bf16[16,1,32,4096]{3,2,1,0:T(8,128)(2,1)} %bitcast.42), calls=%async_computation.1 | async-start | bytes 8388608 | tf_op jit(solution)/shard_map/all_to_all | solution.py:54
where the time goes:
time: 230 us; the launch traced here: 229 us
  blocking collectives  98.7 us (43%)
  waiting for transfers between devices  92.1 us (40%)
  matrix products  27.4 us (12%)
  starting transfers between devices  5.34 us (2%)
  local copies, waits for them, and re-layouts  3.27 us (1%)
  other arithmetic  2.34 us (1%)
    all_to_all x1, blocking collectives, shards(): lax.all_to_all(copies, ('expert', 'tensor'), split_axis=0, concat_axis=0,...  98.7 us
    all_to_all x1, waiting for transfers between devices, shards(): lax.all_to_all(summed, 'expert', split_axis=0, concat_axis=0, tiled=True)  92.1 us
    dot_general x1, matrix products, shards(): jnp.dot(hidden, w_down[0], preferred_element_type=jnp.float32)  16.5 us
    all_to_all x1, starting transfers between devices, shards(): lax.all_to_all(summed, 'expert', split_axis=0, concat_axis=0, tiled=True)  5.34 us
    dot_general x1, matrix products, shards(): jnp.dot(combine_matrix, widened, precision=lax.Precision.HIGHEST, preferr...  5.04 us
  transfers between devices with their start and end apart: 1, of which 1 were waited for; matrix products, arithmetic and copies ran while one was open for 0% of the time, Pallas kernels for 0%

commit v1 on v0

v1 whole, which is shorter than its diff:
```python
import jax
import jax.numpy as jnp
from jax import lax
from jax.sharding import PartitionSpec as P

epsilon = 1e-06
AXES = ("expert", "tensor")


def shards(tokens, norm_gain, w_gate, w_up, w_down, expert_ids, route_weights):
    row_count, feature_count = tokens.shape
    experts = lax.axis_size("expert")
    stream = tokens.astype(jnp.float32)
    normed = (
        stream * lax.rsqrt(jnp.mean(stream * stream, axis=-1, keepdims=True) + epsilon) * norm_gain
    ).astype(jnp.bfloat16)
    route = route_weights / jnp.sum(route_weights, axis=-1, keepdims=True)
    chosen = expert_ids[:, :, None] == jnp.arange(experts, dtype=jnp.int32)[None, None, :]
    table = jnp.sum(jnp.where(chosen, route[:, :, None], 0.0), axis=1)
    tables = lax.all_gather(table, AXES, axis=0, tiled=True)
    rows = lax.all_gather(normed, AXES, axis=0, tiled=True)
    me = lax.axis_index("expert")
    mine = jnp.arange(experts, dtype=jnp.int32)[None, :] == me
    weight = jnp.sum(jnp.where(mine, tables, 0.0), axis=1, keepdims=True)
    gate_pre = jnp.dot(rows, w_gate[0], preferred_element_type=jnp.float32)
    up_pre = jnp.dot(rows, w_up[0], preferred_element_type=jnp.float32)
    hidden = (jax.nn.silu(gate_pre) * up_pre).astype(jnp.bfloat16)
    out = jnp.dot(hidden, w_down[0], preferred_element_type=jnp.float32) * weight
    return lax.psum_scatter(out.astype(jnp.bfloat16), AXES, scatter_dimension=0, tiled=True)


def solution(mesh):
    in_specs = (
        P(("group", "expert", "tensor"), None),
        P(),
        P("expert", None, "tensor"),
        P("expert", None, "tensor"),
        P("expert", "tensor", None),
        P(("group", "expert", "tensor"), None),
        P(("group", "expert", "tensor"), None),
    )
    out_specs = P(("group", "expert", "tensor"), None)
    return jax.shard_map(shards, mesh=mesh, in_specs=in_specs, out_specs=out_specs, check_vma=False)
```

time: 230 us -> 165 us (0.72)
  the two profiles are of different devices: /device:TPU:13 before, /device:TPU:0 now
where the time goes in v1:
time: 165 us
  waiting for transfers between devices  99.1 us (60%)
  blocking collectives  23.6 us (14%)
  matrix products  23.6 us (14%)
  between operations  13.4 us (8%)
  other arithmetic  5.11 us (3%)
    reduce_scatter x1, waiting for transfers between devices, shards(): lax.psum_scatter(out.astype(jnp.bfloat16), AXES, scatter_dimension=0, til...  71.5 us
    all_gather x1, waiting for transfers between devices, shards(): rows = lax.all_gather(normed, AXES, axis=0, tiled=True)  27.5 us
    all_gather x1, blocking collectives, shards(): tables = lax.all_gather(table, AXES, axis=0, tiled=True)  23.6 us
    dot_general x1, matrix products, shards(): jnp.dot(hidden, w_down[0], preferred_element_type=jnp.float32) * weight  16.6 us
    dot_general x1, matrix products, shards(): gate_pre = jnp.dot(rows, w_gate[0], preferred_element_type=jnp.float32)  7.03 us
  transfers between devices with their start and end apart: 2, of which 2 were waited for; matrix products, arithmetic and copies ran while one was open for 1% of the time, Pallas kernels for 0%

profile of v1, /device:TPU:0, one launch (start us, length us, event | category | flops | bytes accessed | tf_op | source)
XLA Modules:
  0.0 165.0 jit_solution(9371344344349594432)
XLA Ops:
  6.5 0.0 all-gather.3.cloned.1.call-start
  6.5 1.1 fusion.9
  7.7 1.8 %fusion.11 = bf16[32,4096]{1,0:T(8,128)(2,1)} fusion(bf16[32,4096]{1,0:T(8,128)(2,1)} %param.7, f32[4096]{0:T(1024)} %param.8, f32[32]{0:T(128)S(1)} %add_rsqrt_fusion), kind=kLoop, calls=%fused_computation.11 | loop fusion | flops 524288 | bytes 540800 | tf_op jit(solution)/shard_map/convert_element_type | solution.py:16
  9.4 0.0 all-gather.3.cloned.1.call-update
  9.5 0.0 reduce-scatter.2.cloned.1.call-start
  9.5 0.7 reduce_sum.37
  10.2 0.7 broadcast_divide_fusion
  10.9 0.7 select_reduce_fusion
  11.6 23.6 %all-gather = f32[16,32,16]{1,2,0:T(8,128)S(1)} all-gather(f32[1,32,16]{1,2,0:T(8,128)S(1)} %bitcast.18), channel_id=1, replica_groups=mesh['group'=2,'expert'=16,'tensor'=1] {'expert','tensor'}, dimensions={0}, use_global_device_ids=true | all-gather | bytes 34816 | tf_op jit(solution)/shard_map/all_gather | solution.py:20
  35.2 0.1 reshape.19
  35.4 0.1 select_reduce_fusion.1
  35.4 27.5 %all-gather.3.cloned.1.call-done = bf16[512,4096]{1,0:T(8,128)(2,1)} async-done(((bf16[32,4096]{1,0:T(8,128)(2,1)}), bf16[512,4096]{1,0:T(8,128)(2,1)}) %all-gather.3.cloned.1.call-update) | async-done | bytes 4194320 | tf_op jit(solution)/shard_map/all_gather | solution.py:21
  63.0 7.0 %fusion.3 = f32[512,768]{1,0:T(8,128)S(1)} fusion(bf16[512,4096]{1,0:T(8,128)(2,1)} %all-gather.3.cloned.1.call-done, bf16[1,4096,768]{2,1,0:T(8,128)(2,1)} %param.9), kind=kOutput, calls=%fused_computation.4 | convolution fusion | flops 3221225472 | bytes 12058624 | tf_op jit(solution)/shard_map/dot_general | solution.py:25
  70.0 16.6 %multiply_convert_fusion = bf16[512,4096]{1,0:T(8,128)(2,1)} fusion(bf16[1,768,4096]{2,1,0:T(8,128)(2,1)} %param.11, f32[512]{0:T(512)S(1)} %select_reduce_fusion.1, f32[512,768]{1,0:T(8,128)S(1)} %fusion.3, bf16[512,4096]{1,0:T(8,128)(2,1)} %all-gather.3.cloned.1.call-done, bf16[1,4096,768]{2,1,0:T(8,128)(2,1)} %param.10), kind=kOutput, calls=%fused_computation | convolution fusion | flops 6449004544 | bytes 22546432 | tf_op jit(solution)/shard_map/dot_general | solution.py:28
  86.6 0.0 reduce-scatter.2.cloned.1.call-update
  86.7 71.5 %reduce-scatter.2.cloned.1.call-done = bf16[32,4096]{1,0:T(8,128)(2,1)} async-done(((bf16[512,4096]{1,0:T(8,128)(2,1)}), bf16[32,4096]{1,0:T(8,128)(2,1)}) %reduce-scatter.2.cloned.1.call-update) | async-done | bytes 262160 | tf_op jit(solution)/shard_map/reduce_scatter | solution.py:29
  (3 shorter events, 0.1 us)
Async XLA Ops:
  6.5 56.5 %all-gather.3.cloned.1.call-start = ((), (), s32[]{:S(2)}) async-start(), calls=%async_computation.1 | async-start | bytes 4456448 | tf_op jit(solution)/shard_map/all_gather | solution.py:21
  9.5 148.7 %reduce-scatter.2.cloned.1.call-start = ((), (), s32[]{:S(2)}) async-start(), calls=%async_computation.2 | async-start | bytes 4456448 | tf_op jit(solution)/shard_map/reduce_scatter | solution.py:29
Sparse Core Ops, SparseCore 0:
  9.6 53.3 all-gather.2
  86.8 71.3 reduce-scatter.1

commit v2 on v1

v2 whole, which is shorter than its diff:
```python
import functools
import jax
import jax.numpy as jnp
from jax import lax
from jax.experimental import pallas as pl
from jax.experimental.pallas import tpu as pltpu
from jax.sharding import PartitionSpec as P

epsilon = 1e-06
AXES = ("expert", "tensor")
MESH = pl.DeviceIdType.MESH
RIGHT, LEFT = 0, 1


class Ring:
    def __init__(self, experts):
        self.pairs = experts // 2
        self.line = self.pairs // 2
        self.group = lax.axis_index("group")
        self.me = lax.axis_index("expert")
        self.core = self.me % 2
        pair = self.me // 2
        row, side = pair // 2, pair % 2
        self.pos = (1 - side) * row + side * (self.pairs - 1 - row)

    def at(self, offset, core=None):
        core = self.core if core is None else core
        place = (self.pos + offset + 2 * self.pairs) % self.pairs
        side = place // self.line
        row = (1 - side) * place + side * (self.pairs - 1 - place)
        return (row * 2 + side) * 2 + core

    def target(self, expert):
        return (self.group, expert, 0)


def meet(ring, partners):
    barrier = pltpu.get_barrier_semaphore()
    for expert in partners:
        pl.semaphore_signal(barrier, inc=1, device_id=ring.target(expert), device_id_type=MESH)
    pl.semaphore_wait(barrier, len(partners))


def remote(ring, src, dst, send_sem, recv_sem, expert):
    return pltpu.make_async_remote_copy(
        src_ref=src,
        dst_ref=dst,
        send_sem=send_sem,
        recv_sem=recv_sem,
        device_id=ring.target(expert),
        device_id_type=MESH,
    )


def runs(direction, half, distance, reach):
    return distance < reach or (distance == reach and half == direction)


def gather_kernel(
    experts, x_ref, t_ref, g_ref, w_ref, ring_send, ring_recv, pair_send, pair_recv, t_send, t_recv, own_sem
):
    ring = Ring(experts)
    reach = ring.pairs // 2
    rows = x_ref.shape[0] // 2
    sibling = ring.at(0, 1 - ring.core)
    peers = [(ring.me + k) % experts for k in range(1, experts)]
    meet(ring, peers)

    def part(ref, h):
        return ref.at[pl.ds(rows * h, rows)]

    def slot(expert, h):
        return g_ref.at[expert, pl.ds(rows * h, rows)]

    sign = (-1, 1)
    sent = []

    def ring_copy(direction, step, h):
        expert = ring.at(sign[direction] * (step - 1))
        src = part(x_ref, h) if step == 1 else slot(expert, h)
        return remote(
            ring,
            src,
            slot(expert, h),
            ring_send.at[direction, step - 1, h],
            ring_recv.at[direction, step - 1, h],
            ring.at(-sign[direction]),
        )

    def ring_arrival(direction, step, h):
        here = slot(ring.at(sign[direction] * step), h)
        return remote(
            ring,
            here,
            here,
            ring_send.at[direction, step - 1, h],
            ring_recv.at[direction, step - 1, h],
            ring.at(-sign[direction]),
        )

    def pair_copy(offset, h):
        expert = ring.at(offset)
        src = part(x_ref, h) if offset == 0 else slot(expert, h)
        index = offset % ring.pairs
        return remote(ring, src, slot(expert, h), pair_send.at[index, h], pair_recv.at[index, h], sibling)

    def pair_arrival(offset, h):
        here = slot(ring.at(offset, 1 - ring.core), h)
        index = offset % ring.pairs
        return remote(ring, here, here, pair_send.at[index, h], pair_recv.at[index, h], sibling)

    def go(copy):
        copy.start()
        sent.append(copy)

    for h in range(2):
        for direction in (RIGHT, LEFT):
            go(ring_copy(direction, 1, h))
    for h in range(2):
        go(pair_copy(0, h))
    for k in range(1, experts):
        to = (ring.me + k) % experts
        go(remote(ring, t_ref.at[to], w_ref.at[ring.me], t_send.at[k - 1], t_recv.at[k - 1], to))
    own = pltpu.make_async_copy(x_ref, g_ref.at[ring.me], own_sem.at[0])
    own.start()
    own_table = pltpu.make_async_copy(t_ref.at[ring.me], w_ref.at[ring.me], own_sem.at[1])
    own_table.start()
    forwarded = [(0, 0), (0, 1)]
    for step in range(1, reach + 1):
        for h in range(2):
            for direction in (RIGHT, LEFT):
                if not runs(direction, h, step, reach):
                    continue
                ring_arrival(direction, step, h).wait_recv()
                if runs(direction, h, step + 1, reach):
                    go(ring_copy(direction, step + 1, h))
                go(pair_copy(sign[direction] * step, h))
                forwarded.append((sign[direction] * step, h))
    for offset, h in forwarded:
        pair_arrival(offset, h).wait_recv()
    for k in range(1, experts):
        origin = (ring.me + experts - k) % experts
        here = w_ref.at[origin]
        remote(ring, here, here, t_send.at[k - 1], t_recv.at[k - 1], origin).wait_recv()
    own.wait()
    own_table.wait()
    for copy in sent:
        copy.wait_send()


def gather_rows(experts, normed, table):
    rows, features = normed.shape
    pairs, reach = experts // 2, experts // 4
    vmem = pl.BlockSpec(memory_space=pltpu.VMEM)
    return pl.pallas_call(
        functools.partial(gather_kernel, experts),
        out_shape=(
            jax.ShapeDtypeStruct((experts, rows, features), normed.dtype),
            jax.ShapeDtypeStruct(table.shape, table.dtype),
        ),
        in_specs=[vmem, vmem],
        out_specs=(vmem, vmem),
        scratch_shapes=[
            pltpu.SemaphoreType.DMA((2, reach, 2)),
            pltpu.SemaphoreType.DMA((2, reach, 2)),
            pltpu.SemaphoreType.DMA((pairs, 2)),
            pltpu.SemaphoreType.DMA((pairs, 2)),
            pltpu.SemaphoreType.DMA((experts - 1,)),
            pltpu.SemaphoreType.DMA((experts - 1,)),
            pltpu.SemaphoreType.DMA((2,)),
        ],
        compiler_params=pltpu.CompilerParams(collective_id=0, has_side_effects=True),
    )(normed, table)


def reduce_kernel(
    experts, p_ref, o_ref, from_pair, landed, leaving, ring_send, ring_recv, pair_send, pair_recv
):
    ring = Ring(experts)
    reach = ring.pairs // 2
    rows = o_ref.shape[0] // 2
    sibling = ring.at(0, 1 - ring.core)
    meet(ring, [ring.at(1), ring.at(-1), sibling])
    toward = (1, -1)

    def cut(ref, index, h):
        return ref.at[index, pl.ds(rows * h, rows)]

    order = []
    for distance in range(reach, -1, -1):
        for h in range(2):
            for direction in (RIGHT, LEFT):
                if distance and runs(direction, h, distance, reach):
                    order.append((direction, distance, h))
    sent = []

    def go(copy):
        copy.start()
        sent.append(copy)

    def pair_copy(offset, h):
        index = offset % ring.pairs
        return remote(
            ring,
            cut(p_ref, ring.at(offset, 1 - ring.core), h),
            cut(from_pair, index, h),
            pair_send.at[index, h],
            pair_recv.at[index, h],
            sibling,
        )

    def ring_copy(direction, distance, h):
        return remote(
            ring,
            leaving.at[direction, distance - 1, pl.ds(rows * h, rows)],
            landed.at[direction, distance - 1, pl.ds(rows * h, rows)],
            ring_send.at[direction, distance - 1, h],
            ring_recv.at[direction, distance - 1, h],
            ring.at(toward[direction]),
        )

    for direction, distance, h in order:
        go(pair_copy(toward[direction] * distance, h))
    for h in range(2):
        go(pair_copy(0, h))
    for direction, distance, h in order:
        offset = toward[direction] * distance
        pair_copy(offset, h).wait_recv()
        span = pl.ds(rows * h, rows)
        total = p_ref[ring.at(offset), span].astype(jnp.float32)
        total = total + from_pair[offset % ring.pairs, span].astype(jnp.float32)
        if runs(direction, h, distance + 1, reach):
            ring_copy(direction, distance + 1, h).wait_recv()
            total = total + landed[direction, distance, span].astype(jnp.float32)
        leaving[direction, distance - 1, span] = total.astype(jnp.bfloat16)
        go(ring_copy(direction, distance, h))
    for h in range(2):
        span = pl.ds(rows * h, rows)
        pair_copy(0, h).wait_recv()
        total = p_ref[ring.me, span].astype(jnp.float32) + from_pair[0, span].astype(jnp.float32)
        for direction in (RIGHT, LEFT):
            ring_copy(direction, 1, h).wait_recv()
            total = total + landed[direction, 0, span].astype(jnp.float32)
        o_ref[span] = total.astype(o_ref.dtype)
    for copy in sent:
        copy.wait_send()


def reduce_rows(experts, pieces):
    _, rows, features = pieces.shape
    pairs, reach = experts // 2, experts // 4
    vmem = pl.BlockSpec(memory_space=pltpu.VMEM)
    return pl.pallas_call(
        functools.partial(reduce_kernel, experts),
        out_shape=jax.ShapeDtypeStruct((rows, features), pieces.dtype),
        in_specs=[vmem],
        out_specs=vmem,
        scratch_shapes=[
            pltpu.VMEM((pairs, rows, features), pieces.dtype),
            pltpu.VMEM((2, reach, rows, features), pieces.dtype),
            pltpu.VMEM((2, reach, rows, features), pieces.dtype),
            pltpu.SemaphoreType.DMA((2, reach, 2)),
            pltpu.SemaphoreType.DMA((2, reach, 2)),
            pltpu.SemaphoreType.DMA((pairs, 2)),
            pltpu.SemaphoreType.DMA((pairs, 2)),
        ],
        compiler_params=pltpu.CompilerParams(collective_id=1, has_side_effects=True),
    )(pieces)


def shards(tokens, norm_gain, w_gate, w_up, w_down, expert_ids, route_weights):
    row_count, feature_count = tokens.shape
    experts = lax.axis_size("expert")
    own_kernels = (
        lax.axis_size("tensor") == 1
        and experts % 4 == 0
        and experts >= 8
        and row_count % 32 == 0
        and row_count <= 128
    )
    stream = tokens.astype(jnp.float32)
    normed = (
        stream * lax.rsqrt(jnp.mean(stream * stream, axis=-1, keepdims=True) + epsilon) * norm_gain
    ).astype(jnp.bfloat16)
    route = route_weights / jnp.sum(route_weights, axis=-1, keepdims=True)
    numbers = jnp.arange(experts, dtype=jnp.int32)
    if own_kernels:
        chosen = expert_ids[None, :, :] == numbers[:, None, None]
        table = jnp.sum(jnp.where(chosen, route[None, :, :], 0.0), axis=2)
        table = jnp.pad(table[:, None, :], ((0, 0), (0, 7), (0, 128 - row_count)))
        rows, weights = gather_rows(experts, normed, table)
        rows = rows.reshape(experts * row_count, feature_count)
        weight = weights[:, 0, :row_count].reshape(-1, 1)
    else:
        chosen = expert_ids[:, :, None] == numbers[None, None, :]
        table = jnp.sum(jnp.where(chosen, route[:, :, None], 0.0), axis=1)
        tables = lax.all_gather(table, AXES, axis=0, tiled=True)
        rows = lax.all_gather(normed, AXES, axis=0, tiled=True)
        mine = numbers[None, :] == lax.axis_index("expert")
        weight = jnp.sum(jnp.where(mine, tables, 0.0), axis=1, keepdims=True)
    gate_pre = jnp.dot(rows, w_gate[0], preferred_element_type=jnp.float32)
    up_pre = jnp.dot(rows, w_up[0], preferred_element_type=jnp.float32)
    hidden = (jax.nn.silu(gate_pre) * up_pre).astype(jnp.bfloat16)
    out = jnp.dot(hidden, w_down[0], preferred_element_type=jnp.float32) * weight
    out = out.astype(jnp.bfloat16)
    if own_kernels:
        return reduce_rows(experts, out.reshape(experts, row_count, feature_count))
    return lax.psum_scatter(out, AXES, scatter_dimension=0, tiled=True)


def solution(mesh):
    in_specs = (
        P(("group", "expert", "tensor"), None),
        P(),
        P("expert", None, "tensor"),
        P("expert", None, "tensor"),
        P("expert", "tensor", None),
        P(("group", "expert", "tensor"), None),
        P(("group", "expert", "tensor"), None),
    )
    out_specs = P(("group", "expert", "tensor"), None)
    return jax.shard_map(shards, mesh=mesh, in_specs=in_specs, out_specs=out_specs, check_vma=False)
```

time: 165 us -> 96.6 us (0.59)
  waiting for transfers between devices: 99.1 us -> 0 us
  Pallas kernels: 0 us -> 64.2 us
  blocking collectives: 23.6 us -> 0 us
  between operations: 13.4 us -> 0.04 us
  local copies, waits for them, and re-layouts: 0.15 us -> 3.26 us
    reduce_scatter x1 -> x0, waiting for transfers between devices: 71.5 us -> none  [shards(): lax.psum_scatter(out.astype(jnp.bfloat16), AXES, scatter_dimension=0, til...]
    pallas_call x0 -> x2, Pallas kernels: none -> 64.2 us  [the longest x1 35.2 us: gather_rows(): pl.pallas_call(functools.partial(gather_kernel, experts), out_shape=(jax....]
    all_gather x1 -> x0, waiting for transfers between devices: 27.5 us -> none  [shards(): rows = lax.all_gather(normed, AXES, axis=0, tiled=True)]
    all_gather x1 -> x0, blocking collectives: 23.6 us -> none  [shards(): tables = lax.all_gather(table, AXES, axis=0, tiled=True)]
  transfers between devices with their start and end apart: 2 -> 0, of which waited for: 2 -> 0; matrix products, arithmetic and copies ran while one was open for 1% -> 0% of each run, Pallas kernels for 0% -> 0%
where the time goes in v2:
time: 96.6 us; the launch traced here: 96.2 us
  Pallas kernels  64.2 us (66%)
  matrix products  23.6 us (24%)
  other arithmetic  5.02 us (5%)
  local copies, waits for them, and re-layouts  3.26 us (3%)
    pallas_call x1, Pallas kernels, gather_rows(): pl.pallas_call(functools.partial(gather_kernel, experts), out_shape=(jax....  35.2 us
    pallas_call x1, Pallas kernels, reduce_rows(): pl.pallas_call(functools.partial(reduce_kernel, experts), out_shape=jax.S...  29 us
    dot_general x1, matrix products, shards(): jnp.dot(hidden, w_down[0], preferred_element_type=jnp.float32) * weight  16.6 us
    dot_general x1, matrix products, shards(): gate_pre = jnp.dot(rows, w_gate[0], preferred_element_type=jnp.float32)  7.04 us

profile of v2, /device:TPU:0, one launch (start us, length us, event | category | flops | bytes accessed | tf_op | source)
XLA Modules:
  0.0 96.2 jit_solution(9919216811513836443)
XLA Ops:
  0.0 1.1 %fusion.9 = f32[32]{0:T(128)S(1)} fusion(bf16[32,4096]{1,0:T(8,128)(2,1)} %param.7), kind=kLoop, calls=%fused_computation.9 | loop fusion | flops 393184 | bytes 262272 | tf_op jit(solution)/shard_map/reduce_sum | solution.py:283
  1.1 0.7 reduce_sum.28
  1.8 0.7 broadcast_divide_fusion
  2.5 0.7 select_reduce_fusion
  3.2 0.6 pad.4.t_ref
  3.9 1.8 %fusion.11.x_ref = bf16[32,4096]{1,0:T(8,128)(2,1)} fusion(bf16[32,4096]{1,0:T(8,128)(2,1)} %param.7, f32[4096]{0:T(1024)} %param.8, f32[32]{0:T(128)S(1)} %add_rsqrt_fusion), kind=kLoop, calls=%fused_computation.11 | loop fusion | flops 524288 | bytes 540800 | tf_op jit(solution)/shard_map/convert_element_type | solution.py:284
  5.7 35.2 %shard_map.73 = (bf16[16,32,4096]{2,1,0:T(8,128)(2,1)}, f32[16,8,128]{2,1,0:T(8,128)}) custom-call(bf16[32,4096]{1,0:T(8,128)(2,1)} %fusion.11.x_ref, f32[16,8,128]{2,1,0:T(8,128)} %pad.4.t_ref), custom_call_target="tpu_custom_call" | custom-call | tf_op jit(solution)/shard_map/pallas_call | solution.py:155
  40.9 0.9 slice_reduce_fusion
  41.7 0.1 mul.43
  41.8 7.0 %fusion.3 = f32[512,768]{1,0:T(8,128)S(1)} fusion(bf16[512,4096]{1,0:T(8,128)(2,1)} %bitcast.20, bf16[1,4096,768]{2,1,0:T(8,128)(2,1)} %param.9), kind=kOutput, calls=%fused_computation.4 | convolution fusion | flops 3221225472 | bytes 12058624 | tf_op jit(solution)/shard_map/dot_general | solution.py:301
  48.9 16.6 %multiply_convert_fusion = bf16[512,4096]{1,0:T(8,128)(2,1)} fusion(bf16[1,768,4096]{2,1,0:T(8,128)(2,1)} %param.11, f32[512]{0:T(512)S(1)} %mul.43, f32[512,768]{1,0:T(8,128)S(1)} %fusion.3, bf16[512,4096]{1,0:T(8,128)(2,1)} %bitcast.21, bf16[1,4096,768]{2,1,0:T(8,128)(2,1)} %param.10), kind=kOutput, calls=%fused_computation | convolution fusion | flops 6449004544 | bytes 22546432 | tf_op jit(solution)/shard_map/dot_general | solution.py:304
  65.5 29.0 %shard_map.74 = bf16[32,4096]{1,0:T(8,128)(2,1)} custom-call(bf16[16,32,4096]{2,1,0:T(8,128)(2,1)} %bitcast.18), custom_call_target="tpu_custom_call" | custom-call | tf_op jit(solution)/shard_map/pallas_call | solution.py:253
  94.5 1.7 %copy.11 = bf16[32,4096]{1,0:T(8,128)(2,1)} copy(bf16[32,4096]{1,0:T(8,128)(2,1)} %shard_map.74) | data formatting | bytes 524288
  (1 shorter events, 0.0 us)

commit v3 on v1

v3 whole, which is shorter than its diff:
```python
import functools
import jax
import jax.numpy as jnp
from jax import lax
from jax.experimental import pallas as pl
from jax.experimental.pallas import tpu as pltpu
from jax.sharding import PartitionSpec as P

epsilon = 1e-06
AXES = ("expert", "tensor")
MESH = pl.DeviceIdType.MESH
RIGHT, LEFT = 0, 1


class Ring:
    def __init__(self, experts):
        self.pairs = experts // 2
        self.line = self.pairs // 2
        self.group = lax.axis_index("group")
        self.me = lax.axis_index("expert")
        self.core = self.me % 2
        pair = self.me // 2
        row, side = pair // 2, pair % 2
        self.pos = (1 - side) * row + side * (self.pairs - 1 - row)

    def at(self, offset, core=None):
        core = self.core if core is None else core
        place = (self.pos + offset + 2 * self.pairs) % self.pairs
        side = place // self.line
        row = (1 - side) * place + side * (self.pairs - 1 - place)
        return (row * 2 + side) * 2 + core

    def target(self, expert):
        return (self.group, expert, 0)


def remote(ring, src, dst, send_sem, recv_sem, expert):
    return pltpu.make_async_remote_copy(
        src_ref=src,
        dst_ref=dst,
        send_sem=send_sem,
        recv_sem=recv_sem,
        device_id=ring.target(expert),
        device_id_type=MESH,
    )


def runs(direction, half, distance, reach):
    return distance < reach or (distance == reach and half == direction)


def slot_of(offset, pairs):
    if offset == 0:
        return 0
    if abs(offset) * 2 == pairs:
        return pairs - 1
    return 2 * abs(offset) - (1 if offset < 0 else 0)


def block_kernel(
    experts,
    x_ref, gain_ref, picks_ref, gate_hbm, up_hbm, down_hbm, o_ref,
    gate, up, down, held, part, hidden, table, weights, from_pair, landed, leaving,
    load_sem, g_send, g_recv, gp_send, gp_recv, t_send, t_recv, r_send, r_recv, rp_send, rp_recv,
):
    ring = Ring(experts)
    pairs = ring.pairs
    reach = pairs // 2
    count, features = x_ref.shape
    ff = gate.shape[1]
    top = picks_ref.shape[0] // 2
    rows = count // 2
    sibling = ring.at(0, 1 - ring.core)
    loads = [
        pltpu.make_async_copy(source.at[0], target, load_sem.at[i])
        for i, (source, target) in enumerate(((gate_hbm, gate), (up_hbm, up), (down_hbm, down)))
    ]
    for load in loads:
        load.start()
    places = [(o, c) for o in range(-reach + 1, reach + 1) for c in range(2) if (o, c) != (0, 0)]
    barrier = pltpu.get_barrier_semaphore()
    for o, c in places:
        peer = ring.target(ring.at(o, (ring.core + c) % 2))
        pl.semaphore_signal(barrier, inc=1, device_id=peer, device_id_type=MESH)

    stream = x_ref[...].astype(jnp.float32)
    scale = lax.rsqrt(jnp.mean(stream * stream, axis=-1, keepdims=True) + epsilon)
    held[0, 0] = (stream * scale * gain_ref[...]).astype(jnp.bfloat16)
    ids = picks_ref[pl.ds(0, top)]
    route = picks_ref[pl.ds(top, top)]
    route = route / jnp.sum(route, axis=0, keepdims=True)
    for e in range(experts):
        table[e] = jnp.sum(jnp.where(ids == e, route, 0.0), axis=0, keepdims=True)
    pl.semaphore_wait(barrier, len(places))

    sent = []

    def go(copy):
        copy.start()
        sent.append(copy)

    def span(h):
        return pl.ds(rows * h, rows)

    came = (-1, 1)

    def held_at(offset, c, h):
        return held.at[slot_of(offset, pairs), c, span(h)]

    def gather_copy(direction, step, h):
        sign = came[direction]
        return remote(
            ring,
            held_at(sign * (step - 1), 0, h),
            held_at(sign * step, 0, h),
            g_send.at[direction, step - 1, h],
            g_recv.at[direction, step - 1, h],
            ring.at(-sign),
        )

    def gather_pair(offset, h):
        index = slot_of(offset, pairs)
        return remote(
            ring,
            held_at(offset, 0, h),
            held_at(offset, 1, h),
            gp_send.at[index, h],
            gp_recv.at[index, h],
            sibling,
        )

    def table_copy(index, o, c):
        expert = ring.at(o, (ring.core + c) % 2)
        back = o if abs(o) * 2 == pairs else -o
        return remote(
            ring,
            table.at[expert],
            weights.at[slot_of(back, pairs), c],
            t_send.at[slot_of(back, pairs), c],
            t_recv.at[slot_of(back, pairs), c],
            expert,
        )

    for h in range(2):
        for direction in (RIGHT, LEFT):
            go(gather_copy(direction, 1, h))
    for h in range(2):
        go(gather_pair(0, h))
    for index, (o, c) in enumerate(places):
        go(table_copy(index, o, c))

    def column(slot, c):
        line = table[ring.me] if (slot, c) == (0, 0) else weights[slot, c]
        square = jnp.broadcast_to(line, (count, count))
        same = lax.broadcasted_iota(jnp.int32, (count, count), 0) == lax.broadcasted_iota(
            jnp.int32, (count, count), 1
        )
        return jnp.sum(jnp.where(same, square, 0.0), axis=1, keepdims=True)

    def compute(first, slots):
        tall = slots * 2 * count
        hidden_tile, out_tile = 256, 512

        @pl.loop(0, ff // hidden_tile)
        def _(i):
            columns = pl.ds(pl.multiple_of(i * hidden_tile, hidden_tile), hidden_tile)
            block = held[pl.ds(first, slots)].reshape(tall, features)
            pre = jnp.dot(block, gate[:, columns], preferred_element_type=jnp.float32)
            lift = jnp.dot(block, up[:, columns], preferred_element_type=jnp.float32)
            hidden[pl.ds(0, tall), columns] = (pre / (1.0 + jnp.exp(-pre)) * lift).astype(jnp.bfloat16)

        if first == 0:
            loads[2].wait()
        for o, c in places:
            if first <= slot_of(o, pairs) < first + slots:
                index = slot_of(o, pairs)
                remote(
                    ring,
                    weights.at[index, c],
                    weights.at[index, c],
                    t_send.at[index, c],
                    t_recv.at[index, c],
                    sibling,
                ).wait_recv()
        weight = jnp.concatenate([column(first + j, c) for j in range(slots) for c in range(2)], axis=0)

        @pl.loop(0, features // out_tile)
        def _(i):
            columns = pl.ds(pl.multiple_of(i * out_tile, out_tile), out_tile)
            out = jnp.dot(hidden[pl.ds(0, tall)], down[:, columns], preferred_element_type=jnp.float32)
            out = (out * weight).astype(jnp.bfloat16).reshape(slots, 2, count, out_tile)
            part[pl.ds(first, slots), :, :, columns] = out

    toward = (1, -1)

    def reduce_pair(offset, h):
        index = slot_of(offset, pairs)
        return remote(
            ring,
            part.at[index, 1, span(h)],
            from_pair.at[index, span(h)],
            rp_send.at[index, h],
            rp_recv.at[index, h],
            sibling,
        )

    def reduce_copy(direction, distance, h):
        return remote(
            ring,
            leaving.at[direction, distance - 1, span(h)],
            landed.at[direction, distance - 1, span(h)],
            r_send.at[direction, distance - 1, h],
            r_recv.at[direction, distance - 1, h],
            ring.at(toward[direction]),
        )

    def lanes(distance):
        if distance == 0:
            return [(RIGHT, 0), (RIGHT, 1)]
        return [(d, h) for h in range(2) for d in (RIGHT, LEFT) if runs(d, h, distance, reach)]

    def settle(distance):
        for direction, h in lanes(distance):
            gather_pair(came[direction] * distance, h).wait_recv()
        if distance == 0:
            loads[0].wait()
            loads[1].wait()
        first = 0 if distance == 0 else 2 * distance - 1
        compute(first, 1 if distance in (0, reach) else 2)
        for direction, h in lanes(distance):
            go(reduce_pair(toward[direction] * distance, h))

    def pass_on(distance):
        for direction, h in lanes(distance):
            index = slot_of(toward[direction] * distance, pairs)
            reduce_pair(toward[direction] * distance, h).wait_recv()
            total = part[index, 0, span(h)].astype(jnp.float32)
            total = total + from_pair[index, span(h)].astype(jnp.float32)
            if runs(direction, h, distance + 1, reach):
                reduce_copy(direction, distance + 1, h).wait_recv()
                total = total + landed[direction, distance, span(h)].astype(jnp.float32)
            leaving[direction, distance - 1, span(h)] = total.astype(jnp.bfloat16)
            go(reduce_copy(direction, distance, h))

    for step in range(1, reach + 1):
        for direction, h in lanes(step):
            gather_copy(direction, step, h).wait_recv()
            if runs(direction, h, step + 1, reach):
                go(gather_copy(direction, step + 1, h))
            go(gather_pair(came[direction] * step, h))
        if step < reach:
            settle(step - 1)
    settle(reach)
    pass_on(reach)
    settle(reach - 1)
    for distance in range(reach - 1, 0, -1):
        pass_on(distance)
    for h in range(2):
        reduce_pair(0, h).wait_recv()
        total = part[0, 0, span(h)].astype(jnp.float32) + from_pair[0, span(h)].astype(jnp.float32)
        for direction in (RIGHT, LEFT):
            reduce_copy(direction, 1, h).wait_recv()
            total = total + landed[direction, 0, span(h)].astype(jnp.float32)
        o_ref[span(h)] = total.astype(o_ref.dtype)
    for copy in sent:
        copy.wait_send()


def expert_block(experts, tokens, gain, picks, w_gate, w_up, w_down):
    count, features = tokens.shape
    ff = w_gate.shape[2]
    pairs, reach = experts // 2, experts // 4
    bf16, f32 = jnp.bfloat16, jnp.float32
    dma = pltpu.SemaphoreType.DMA
    vmem = pl.BlockSpec(memory_space=pltpu.VMEM)
    anywhere = pl.BlockSpec(memory_space=pl.ANY)
    return pl.pallas_call(
        functools.partial(block_kernel, experts),
        out_shape=jax.ShapeDtypeStruct((count, features), bf16),
        in_specs=[vmem, vmem, vmem, anywhere, anywhere, anywhere],
        out_specs=vmem,
        scratch_shapes=[
            pltpu.VMEM((features, ff), bf16),
            pltpu.VMEM((features, ff), bf16),
            pltpu.VMEM((ff, features), bf16),
            pltpu.VMEM((pairs, 2, count, features), bf16),
            pltpu.VMEM((pairs, 2, count, features), bf16),
            pltpu.VMEM((4 * count, ff), bf16),
            pltpu.VMEM((experts, 1, count), f32),
            pltpu.VMEM((pairs, 2, 1, count), f32),
            pltpu.VMEM((pairs, count, features), bf16),
            pltpu.VMEM((2, reach, count, features), bf16),
            pltpu.VMEM((2, reach, count, features), bf16),
            dma((3,)),
            dma((2, reach, 2)),
            dma((2, reach, 2)),
            dma((pairs, 2)),
            dma((pairs, 2)),
            dma((pairs, 2)),
            dma((pairs, 2)),
            dma((2, reach, 2)),
            dma((2, reach, 2)),
            dma((pairs, 2)),
            dma((pairs, 2)),
        ],
        compiler_params=pltpu.CompilerParams(
            collective_id=0, has_side_effects=True, vmem_limit_bytes=60 * 1024 * 1024
        ),
    )(tokens, gain, picks, w_gate, w_up, w_down)


def shards(tokens, norm_gain, w_gate, w_up, w_down, expert_ids, route_weights):
    row_count, feature_count = tokens.shape
    experts = lax.axis_size("expert")
    own_kernels = (
        lax.axis_size("tensor") == 1
        and experts % 4 == 0
        and experts >= 8
        and row_count % 32 == 0
        and row_count <= 32
        and w_gate.shape[2] % 256 == 0
        and feature_count % 512 == 0
    )
    if own_kernels:
        picks = jnp.concatenate([expert_ids.astype(jnp.float32), route_weights], axis=1).T
        return expert_block(experts, tokens, norm_gain[None, :], picks, w_gate, w_up, w_down)
    stream = tokens.astype(jnp.float32)
    normed = (
        stream * lax.rsqrt(jnp.mean(stream * stream, axis=-1, keepdims=True) + epsilon) * norm_gain
    ).astype(jnp.bfloat16)
    route = route_weights / jnp.sum(route_weights, axis=-1, keepdims=True)
    numbers = jnp.arange(experts, dtype=jnp.int32)
    chosen = expert_ids[:, :, None] == numbers[None, None, :]
    table = jnp.sum(jnp.where(chosen, route[:, :, None], 0.0), axis=1)
    tables = lax.all_gather(table, AXES, axis=0, tiled=True)
    rows = lax.all_gather(normed, AXES, axis=0, tiled=True)
    mine = numbers[None, :] == lax.axis_index("expert")
    weight = jnp.sum(jnp.where(mine, tables, 0.0), axis=1, keepdims=True)
    gate_pre = jnp.dot(rows, w_gate[0], preferred_element_type=jnp.float32)
    up_pre = jnp.dot(rows, w_up[0], preferred_element_type=jnp.float32)
    hidden = (jax.nn.silu(gate_pre) * up_pre).astype(jnp.bfloat16)
    out = jnp.dot(hidden, w_down[0], preferred_element_type=jnp.float32) * weight
    out = out.astype(jnp.bfloat16)
    return lax.psum_scatter(out, AXES, scatter_dimension=0, tiled=True)


def solution(mesh):
    in_specs = (
        P(("group", "expert", "tensor"), None),
        P(),
        P("expert", None, "tensor"),
        P("expert", None, "tensor"),
        P("expert", "tensor", None),
        P(("group", "expert", "tensor"), None),
        P(("group", "expert", "tensor"), None),
    )
    out_specs = P(("group", "expert", "tensor"), None)
    return jax.shard_map(shards, mesh=mesh, in_specs=in_specs, out_specs=out_specs, check_vma=False)
```

time: 165 us -> 68.8 us (0.42)
  waiting for transfers between devices: 99.1 us -> 0 us
  Pallas kernels: 0 us -> 64.9 us
  matrix products: 23.6 us -> 0 us
  blocking collectives: 23.6 us -> 0 us
  between operations: 13.4 us -> 0.01 us
  other arithmetic: 5.11 us -> 1.98 us
    reduce_scatter x1 -> x0, waiting for transfers between devices: 71.5 us -> none  [shards(): lax.psum_scatter(out.astype(jnp.bfloat16), AXES, scatter_dimension=0, til...]
    pallas_call x0 -> x1, Pallas kernels: none -> 64.9 us  [expert_block(): pl.pallas_call(functools.partial(block_kernel, experts), out_shape=jax.Sh...]
    all_gather x1 -> x0, waiting for transfers between devices: 27.5 us -> none  [shards(): rows = lax.all_gather(normed, AXES, axis=0, tiled=True)]
    dot_general x2 -> x0, matrix products: 23.6 us -> none  [the longest x1 16.6 us: shards(): jnp.dot(hidden, w_down[0], preferred_element_type=jnp.float32) * weight]
    all_gather x1 -> x0, blocking collectives: 23.6 us -> none  [shards(): tables = lax.all_gather(table, AXES, axis=0, tiled=True)]
    reduce_sum x4 -> x0, other arithmetic: 2.61 us -> none  [the longest x1 1.11 us: shards(): jnp.mean(stream * stream, axis=-1, keepdims=True) + epsilon]
  transfers between devices with their start and end apart: 2 -> 0, of which waited for: 2 -> 0; matrix products, arithmetic and copies ran while one was open for 1% -> 0% of each run, Pallas kernels for 0% -> 0%
where the time goes in v3:
time: 68.8 us; the launch traced here: 68.6 us
  Pallas kernels  64.9 us (94%)
  other arithmetic  1.98 us (3%)
  local copies, waits for them, and re-layouts  1.67 us (2%)
    pallas_call x1, Pallas kernels, expert_block(): pl.pallas_call(functools.partial(block_kernel, experts), out_shape=jax.Sh...  64.9 us
    unnamed x1, local copies, waits for them, and re-layouts  1.67 us

profile of v3, /device:TPU:0, one launch (start us, length us, event | category | flops | bytes accessed | tf_op | source)
XLA Modules:
  0.0 68.6 jit_solution(12798738110341756472)
XLA Ops:
  0.0 0.7 %convert_element_type.3 = f32[32,8]{0,1:T(8,128)S(1)} convert(s32[32,8]{0,1:T(8,128)} %param.12) | non-fusion elementwise | flops 256 | bytes 2048 | tf_op jit(solution)/shard_map/convert_element_type | solution.py:325
  0.7 1.3 %maximum_bitcast_fusion.picks_ref = f32[16,32]{1,0:T(8,128)} fusion(f32[32,8]{0,1:T(8,128)} %param.13, f32[32,8]{0,1:T(8,128)S(1)} %convert_element_type.3), kind=kLoop, calls=%fused_computation | loop fusion | flops 512 | bytes 4096 | tf_op jit(solution)/shard_map/transpose | solution.py:325
  2.0 64.9 %shard_map.73 = bf16[32,4096]{1,0:T(8,128)(2,1)} custom-call(bf16[32,4096]{1,0:T(8,128)(2,1)} %x_ref.1, f32[1,4096]{1,0:T(1,128)} %bitcast.3, f32[16,32]{1,0:T(8,128)} %maximum_bitcast_fusion.picks_ref, bf16[1,4096,768]{2,1,0:T(8,128)(2,1)} %gate_hbm.1, bf16[1,4096,768]{2,1,0:T(8,128)(2,1)} %up_hbm.1, bf16[1,768,4096]{2,1,0:T(8,128)(2,1)} %down_hbm.1), custom_call_target="tpu_custom_call" | custom-call | tf_op jit(solution)/shard_map/pallas_call | solution.py:277
  66.9 1.7 %copy.9 = bf16[32,4096]{1,0:T(8,128)(2,1)} copy(bf16[32,4096]{1,0:T(8,128)(2,1)} %shard_map.73) | data formatting | bytes 524288

commit v4 on v3

--- a/solution.py
+++ b/solution.py
@@ -59,16 +59,15 @@
 
 def block_kernel(
     experts,
-    x_ref, gain_ref, picks_ref, gate_hbm, up_hbm, down_hbm, o_ref,
-    gate, up, down, held, part, hidden, table, weights, from_pair, landed, leaving,
-    load_sem, g_send, g_recv, gp_send, gp_recv, t_send, t_recv, r_send, r_recv, rp_send, rp_recv,
+    x_ref, gain_ref, ids_ref, route_ref, gate_hbm, up_hbm, down_hbm, o_ref,
+    gate, up, down, held, part, hidden, table, from_pair, landed, leaving,
+    load_sem, g_send, g_recv, gp_send, gp_recv, t_send, t_recv, tp_send, tp_recv, r_send, r_recv, rp_send, rp_recv,
 ):
     ring = Ring(experts)
     pairs = ring.pairs
     reach = pairs // 2
     count, features = x_ref.shape
     ff = gate.shape[1]
-    top = picks_ref.shape[0] // 2
     rows = count // 2
     sibling = ring.at(0, 1 - ring.core)
     loads = [
@@ -77,21 +76,14 @@
     ]
     for load in loads:
         load.start()
-    places = [(o, c) for o in range(-reach + 1, reach + 1) for c in range(2) if (o, c) != (0, 0)]
     barrier = pltpu.get_barrier_semaphore()
-    for o, c in places:
-        peer = ring.target(ring.at(o, (ring.core + c) % 2))
-        pl.semaphore_signal(barrier, inc=1, device_id=peer, device_id_type=MESH)
+    for partner in (ring.at(1), ring.at(-1), sibling):
+        pl.semaphore_signal(barrier, inc=1, device_id=ring.target(partner), device_id_type=MESH)
 
     stream = x_ref[...].astype(jnp.float32)
     scale = lax.rsqrt(jnp.mean(stream * stream, axis=-1, keepdims=True) + epsilon)
     held[0, 0] = (stream * scale * gain_ref[...]).astype(jnp.bfloat16)
-    ids = picks_ref[pl.ds(0, top)]
-    route = picks_ref[pl.ds(top, top)]
-    route = route / jnp.sum(route, axis=0, keepdims=True)
-    for e in range(experts):
-        table[e] = jnp.sum(jnp.where(ids == e, route, 0.0), axis=0, keepdims=True)
-    pl.semaphore_wait(barrier, len(places))
+    pl.semaphore_wait(barrier, 3)
 
     sent = []
 
@@ -129,35 +121,42 @@
             sibling,
         )
 
-    def table_copy(index, o, c):
-        expert = ring.at(o, (ring.core + c) % 2)
-        back = o if abs(o) * 2 == pairs else -o
-        return remote(
-            ring,
-            table.at[expert],
-            weights.at[slot_of(back, pairs), c],
-            t_send.at[slot_of(back, pairs), c],
-            t_recv.at[slot_of(back, pairs), c],
-            expert,
-        )
+    def table_copy(direction, step):
+        sign = came[direction]
+        return remote(
+            ring,
+            table.at[slot_of(sign * (step - 1), pairs), 0],
+            table.at[slot_of(sign * step, pairs), 0],
+            t_send.at[direction, step - 1],
+            t_recv.at[direction, step - 1],
+            ring.at(-sign),
+        )
+
+    def table_pair(offset):
+        index = slot_of(offset, pairs)
+        return remote(ring, table.at[index, 0], table.at[index, 1], tp_send.at[index], tp_recv.at[index], sibling)
 
     for h in range(2):
         for direction in (RIGHT, LEFT):
             go(gather_copy(direction, 1, h))
     for h in range(2):
         go(gather_pair(0, h))
-    for index, (o, c) in enumerate(places):
-        go(table_copy(index, o, c))
+    lane = lax.broadcasted_iota(jnp.int32, (count, experts), 1)
+    ids = ids_ref[...]
+    route = route_ref[...]
+    route = route / jnp.sum(route, axis=1, keepdims=True)
+    spread = jnp.zeros((count, experts), jnp.float32)
+    for k in range(ids_ref.shape[1]):
+        spread = spread + jnp.where(ids[:, k : k + 1] == lane, route[:, k : k + 1], 0.0)
+    table[0, 0] = spread
+    for direction in (RIGHT, LEFT):
+        go(table_copy(direction, 1))
+    go(table_pair(0))
 
     def column(slot, c):
-        line = table[ring.me] if (slot, c) == (0, 0) else weights[slot, c]
-        square = jnp.broadcast_to(line, (count, count))
-        same = lax.broadcasted_iota(jnp.int32, (count, count), 0) == lax.broadcasted_iota(
-            jnp.int32, (count, count), 1
-        )
-        return jnp.sum(jnp.where(same, square, 0.0), axis=1, keepdims=True)
-
-    def compute(first, slots):
+        return jnp.sum(jnp.where(lane == ring.me, table[slot, c], 0.0), axis=1, keepdims=True)
+
+    def compute(first, slots, between):
         tall = slots * 2 * count
         hidden_tile, out_tile = 256, 512
 
@@ -169,19 +168,9 @@
             lift = jnp.dot(block, up[:, columns], preferred_element_type=jnp.float32)
             hidden[pl.ds(0, tall), columns] = (pre / (1.0 + jnp.exp(-pre)) * lift).astype(jnp.bfloat16)
 
+        between()
         if first == 0:
             loads[2].wait()
-        for o, c in places:
-            if first <= slot_of(o, pairs) < first + slots:
-                index = slot_of(o, pairs)
-                remote(
-                    ring,
-                    weights.at[index, c],
-                    weights.at[index, c],
-                    t_send.at[index, c],
-                    t_recv.at[index, c],
-                    sibling,
-                ).wait_recv()
         weight = jnp.concatenate([column(first + j, c) for j in range(slots) for c in range(2)], axis=0)
 
         @pl.loop(0, features // out_tile)
@@ -219,14 +208,19 @@
             return [(RIGHT, 0), (RIGHT, 1)]
         return [(d, h) for h in range(2) for d in (RIGHT, LEFT) if runs(d, h, distance, reach)]
 
-    def settle(distance):
+    def offsets(distance):
+        return (distance,) if distance in (0, reach) else (-distance, distance)
+
+    def settle(distance, between=lambda: None):
         for direction, h in lanes(distance):
             gather_pair(came[direction] * distance, h).wait_recv()
+        for offset in offsets(distance):
+            table_pair(offset).wait_recv()
         if distance == 0:
             loads[0].wait()
             loads[1].wait()
         first = 0 if distance == 0 else 2 * distance - 1
-        compute(first, 1 if distance in (0, reach) else 2)
+        compute(first, 1 if distance in (0, reach) else 2, between)
         for direction, h in lanes(distance):
             go(reduce_pair(toward[direction] * distance, h))
 
@@ -242,14 +236,28 @@
             leaving[direction, distance - 1, span(h)] = total.astype(jnp.bfloat16)
             go(reduce_copy(direction, distance, h))
 
-    for step in range(1, reach + 1):
+    def forward(step, half):
         for direction, h in lanes(step):
+            if h != half:
+                continue
             gather_copy(direction, step, h).wait_recv()
             if runs(direction, h, step + 1, reach):
                 go(gather_copy(direction, step + 1, h))
             go(gather_pair(came[direction] * step, h))
-        if step < reach:
-            settle(step - 1)
+            if h == 0 and not (step == reach and direction == LEFT):
+                table_copy(direction, step).wait_recv()
+                if step + 1 < reach or (step + 1 == reach and direction == RIGHT):
+                    go(table_copy(direction, step + 1))
+                go(table_pair(came[direction] * step))
+
+    forward(1, 0)
+    forward(1, 1)
+    settle(0)
+    for step in range(2, reach):
+        forward(step, 0)
+        settle(step - 1, functools.partial(forward, step, 1))
+    forward(reach, 0)
+    forward(reach, 1)
     settle(reach)
     pass_on(reach)
     settle(reach - 1)
@@ -266,7 +274,7 @@
         copy.wait_send()
 
 
-def expert_block(experts, tokens, gain, picks, w_gate, w_up, w_down):
+def expert_block(experts, tokens, gain, ids, route, w_gate, w_up, w_down):
     count, features = tokens.shape
     ff = w_gate.shape[2]
     pairs, reach = experts // 2, experts // 4
@@ -277,7 +285,7 @@
     return pl.pallas_call(
         functools.partial(block_kernel, experts),
         out_shape=jax.ShapeDtypeStruct((count, features), bf16),
-        in_specs=[vmem, vmem, vmem, anywhere, anywhere, anywhere],
+        in_specs=[vmem, vmem, vmem, vmem, anywhere, anywhere, anywhere],
         out_specs=vmem,
         scratch_shapes=[
             pltpu.VMEM((features, ff), bf16),
@@ -286,8 +294,7 @@
             pltpu.VMEM((pairs, 2, count, features), bf16),
             pltpu.VMEM((pairs, 2, count, features), bf16),
             pltpu.VMEM((4 * count, ff), bf16),
-            pltpu.VMEM((experts, 1, count), f32),
-            pltpu.VMEM((pairs, 2, 1, count), f32),
+            pltpu.VMEM((pairs, 2, count, experts), f32),
             pltpu.VMEM((pairs, count, features), bf16),
             pltpu.VMEM((2, reach, count, features), bf16),
             pltpu.VMEM((2, reach, count, features), bf16),
@@ -296,8 +303,10 @@
             dma((2, reach, 2)),
             dma((pairs, 2)),
             dma((pairs, 2)),
-            dma((pairs, 2)),
-            dma((pairs, 2)),
+            dma((2, reach)),
+            dma((2, reach)),
+            dma((pairs,)),
+            dma((pairs,)),
             dma((2, reach, 2)),
             dma((2, reach, 2)),
             dma((pairs, 2)),
@@ -306,7 +315,7 @@
         compiler_params=pltpu.CompilerParams(
             collective_id=0, has_side_effects=True, vmem_limit_bytes=60 * 1024 * 1024
         ),
-    )(tokens, gain, picks, w_gate, w_up, w_down)
+    )(tokens, gain, ids, route, w_gate, w_up, w_down)
 
 
 def shards(tokens, norm_gain, w_gate, w_up, w_down, expert_ids, route_weights):
@@ -322,8 +331,7 @@
         and feature_count % 512 == 0
     )
     if own_kernels:
-        picks = jnp.concatenate([expert_ids.astype(jnp.float32), route_weights], axis=1).T
-        return expert_block(experts, tokens, norm_gain[None, :], picks, w_gate, w_up, w_down)
+        return expert_block(experts, tokens, norm_gain[None, :], expert_ids, route_weights, w_gate, w_up, w_down)
     stream = tokens.astype(jnp.float32)
     normed = (
         stream * lax.rsqrt(jnp.mean(stream * stream, axis=-1, keepdims=True) + epsilon) * norm_gain

time: 68.8 us -> 68.2 us (level)
  local copies, waits for them, and re-layouts: 1.67 us -> 4.39 us
  other arithmetic: 1.98 us -> 0 us
  Pallas kernels: 64.9 us -> 63.6 us
    unnamed x1 -> x3, local copies, waits for them, and re-layouts: 1.67 us -> 4.39 us
    pallas_call x1, Pallas kernels: 64.9 us -> 63.6 us  [expert_block(): pl.pallas_call(functools.partial(block_kernel, experts), out_shape=jax.Sh...]
    transpose x1 -> x0, other arithmetic: 1.29 us -> none  [shards(): jnp.concatenate([expert_ids.astype(jnp.float32), route_weights], axis=1)]
    convert_element_type x1 -> x0, other arithmetic: 0.69 us -> none  [shards(): expert_ids.astype(jnp.float32)]
where the time goes in v4:
time: 68.2 us; the launch traced here: 68 us
  Pallas kernels  63.6 us (93%)
  local copies, waits for them, and re-layouts  4.39 us (6%)
    pallas_call x1, Pallas kernels, expert_block(): pl.pallas_call(functools.partial(block_kernel, experts), out_shape=jax.Sh...  63.6 us
    unnamed x3, local copies, waits for them, and re-layouts  4.39 us

profile of v4, /device:TPU:0, one launch (start us, length us, event | category | flops | bytes accessed | tf_op | source)
XLA Modules:
  0.0 68.0 jit_solution(10952255425298110210)
XLA Ops:
  0.0 1.4 %copy.8.ids_ref = s32[32,8]{1,0:T(8,128)} copy(s32[32,8]{0,1:T(8,128)} %param.12) | data formatting | bytes 2048 | tf_op args[5]
  1.4 1.4 %copy.9.route_ref = f32[32,8]{1,0:T(8,128)} copy(f32[32,8]{0,1:T(8,128)} %param.13) | data formatting | bytes 2048 | tf_op args[6]
  2.7 63.6 %shard_map.73 = bf16[32,4096]{1,0:T(8,128)(2,1)} custom-call(bf16[32,4096]{1,0:T(8,128)(2,1)} %x_ref.1, f32[1,4096]{1,0:T(1,128)} %bitcast.1, s32[32,8]{1,0:T(8,128)} %copy.8.ids_ref, f32[32,8]{1,0:T(8,128)} %copy.9.route_ref, bf16[1,4096,768]{2,1,0:T(8,128)(2,1)} %gate_hbm.1, bf16[1,4096,768]{2,1,0:T(8,128)(2,1)} %up_hbm.1, bf16[1,768,4096]{2,1,0:T(8,128)(2,1)} %down_hbm.1), custom_call_target="tpu_custom_call" | custom-call | tf_op jit(solution)/shard_map/pallas_call | solution.py:285
  66.3 1.7 %copy.11 = bf16[32,4096]{1,0:T(8,128)(2,1)} copy(bf16[32,4096]{1,0:T(8,128)(2,1)} %shard_map.73) | data formatting | bytes 524288

commit v5 on v4

--- a/solution.py
+++ b/solution.py
@@ -142,12 +142,19 @@
     for h in range(2):
         go(gather_pair(0, h))
     lane = lax.broadcasted_iota(jnp.int32, (count, experts), 1)
-    ids = ids_ref[...]
+    square = (count, count)
+    same = lax.broadcasted_iota(jnp.int32, square, 0) == lax.broadcasted_iota(jnp.int32, square, 1)
+
+    def upright(line):
+        return jnp.sum(jnp.where(same, jnp.broadcast_to(line, square), 0.0), axis=1, keepdims=True)
+
+    ids = ids_ref[...].astype(jnp.float32)
     route = route_ref[...]
-    route = route / jnp.sum(route, axis=1, keepdims=True)
+    route = route / jnp.sum(route, axis=0, keepdims=True)
     spread = jnp.zeros((count, experts), jnp.float32)
-    for k in range(ids_ref.shape[1]):
-        spread = spread + jnp.where(ids[:, k : k + 1] == lane, route[:, k : k + 1], 0.0)
+    for k in range(ids_ref.shape[0]):
+        hit = upright(ids[k : k + 1]) == lane.astype(jnp.float32)
+        spread = spread + jnp.where(hit, upright(route[k : k + 1]), 0.0)
     table[0, 0] = spread
     for direction in (RIGHT, LEFT):
         go(table_copy(direction, 1))
@@ -331,7 +338,8 @@
         and feature_count % 512 == 0
     )
     if own_kernels:
-        return expert_block(experts, tokens, norm_gain[None, :], expert_ids, route_weights, w_gate, w_up, w_down)
+        ids, route = expert_ids.T, route_weights.T
+        return expert_block(experts, tokens, norm_gain[None, :], ids, route, w_gate, w_up, w_down)
     stream = tokens.astype(jnp.float32)
     normed = (
         stream * lax.rsqrt(jnp.mean(stream * stream, axis=-1, keepdims=True) + epsilon) * norm_gain

time: 68.2 us -> 65.4 us (0.959)
  local copies, waits for them, and re-layouts: 4.39 us -> 1.67 us
    unnamed x3 -> x1, local copies, waits for them, and re-layouts: 4.39 us -> 1.67 us
where the time goes in v5:
time: 65.4 us; the launch traced here: 65.3 us
  Pallas kernels  63.6 us (97%)
  local copies, waits for them, and re-layouts  1.67 us (3%)
    pallas_call x1, Pallas kernels, expert_block(): pl.pallas_call(functools.partial(block_kernel, experts), out_shape=jax.Sh...  63.6 us
    unnamed x1, local copies, waits for them, and re-layouts  1.67 us

profile of v5, /device:TPU:0, one launch (start us, length us, event | category | flops | bytes accessed | tf_op | source)
XLA Modules:
  0.0 65.3 jit_solution(8969520800674416132)
XLA Ops:
  0.0 63.6 %shard_map.73 = bf16[32,4096]{1,0:T(8,128)(2,1)} custom-call(bf16[32,4096]{1,0:T(8,128)(2,1)} %x_ref.1, f32[1,4096]{1,0:T(1,128)} %bitcast.3, s32[8,32]{1,0:T(8,128)} %bitcast.4, f32[8,32]{1,0:T(8,128)} %bitcast.5, bf16[1,4096,768]{2,1,0:T(8,128)(2,1)} %gate_hbm.1, bf16[1,4096,768]{2,1,0:T(8,128)(2,1)} %up_hbm.1, bf16[1,768,4096]{2,1,0:T(8,128)(2,1)} %down_hbm.1), custom_call_target="tpu_custom_call" | custom-call | tf_op jit(solution)/shard_map/pallas_call | solution.py:292
  63.6 1.7 %copy.9 = bf16[32,4096]{1,0:T(8,128)(2,1)} copy(bf16[32,4096]{1,0:T(8,128)(2,1)} %shard_map.73) | data formatting | bytes 524288
